TPU v7x, 256 devices: a whole 4x4x8 slice. The times are simulated.
256 devices in a mesh: leaf: 64 (over y, z, core), grid: 4 (over x).
Axes of the slice: x: 4, y: 4, z: 8, core: 2. Of those that a mesh axis runs over, the one named last changes fastest.
Arguments:
- rhs: bfloat16 [5, 128, 256, 256], P(None, 'leaf', 'grid'), may hold values from -6 to 6
- fwd_inv: bfloat16 [5, 128, 256, 256], P(None, 'leaf', 'grid')
- bwd_inv: bfloat16 [5, 128, 256, 256], P(None, 'leaf', 'grid')
- upd_t: bfloat16 [4, 128, 256, 512], P(None, 'leaf', 'grid'), may hold values from -0.25 to 0.25
- bwd_t: bfloat16 [4, 128, 512, 256], P(None, 'leaf', 'grid'), may hold values from -0.1875 to 0.1875
- dest_owner: int32 [4, 64, 4, 256, 1], P(None, 'leaf', 'grid'), may hold values from 0 to 63; in each aligned block of 256 rows (0 to 255, 256 to 511, ..., all dimensions but the last counted through in order) at most 10 rows name the same one
- dest_row: int32 [4, 64, 4, 256], P(None, 'leaf', 'grid'), may hold values from 128 to 639, as said below
Outputs:
- solution: bfloat16 [5, 128, 256, 256], P(None, 'leaf', 'grid')
Inputs may be any that keep to these rules, and one draw needn't show every extreme that they name: `dest_owner`: in the rows of one device at one level (one aligned block of 256), no owner is named more than 10 times, a bound that some block reaches. `dest_row`: an entry of level l reaches a row of a later level: it lies from (l + 1) * 2 * 64 to 639.
All inputs are finite; a program needn't handle non-finite values.
Results may differ from a plain program's by a relative error of at most 0.025.
Values may be sent and summed in bfloat16 or wider, within the bound.
A program may use at most 64 MiB of HBM per device.

v0:
```python
import jax
import jax.numpy as jnp
from jax import lax
from jax.sharding import PartitionSpec as P


def apply_inverse(inverse_rows, block_bf):
    return jnp.einsum(
        "kiw,kwn->kin",
        inverse_rows,
        lax.all_gather(block_bf, "grid", axis=1, tiled=True),
        preferred_element_type=jnp.float32,
    )


def grid_reduce(term_fn, kept_rows):
    return lax.psum_scatter(
        term_fn(jnp.int32(0), kept_rows * lax.axis_size("grid")).astype(jnp.bfloat16),
        "grid",
        scatter_dimension=0,
        tiled=True,
    ).astype(jnp.float32)


def send_back(solved_rows):
    return lax.all_to_all(solved_rows, "leaf", split_axis=0, concat_axis=0, tiled=True)


def local(rhs, fwd_inv, bwd_inv, upd_t, bwd_t, dest_owner, dest_row):
    levels, per_level, grid_rows, columns = rhs.shape
    group_rows = bwd_t.shape[2]
    owners = lax.axis_size("leaf")
    capacity = max(2, 8 * per_level * group_rows // (3 * owners))
    block_rows = per_level * grid_rows
    leaf_ids = jnp.arange(owners, dtype=jnp.int32)
    accum = rhs.astype(jnp.float32).reshape(levels * block_rows, columns)

    def placement(level):
        owner_ids = dest_owner[level].reshape(-1)
        targets = dest_row[level].reshape(-1)
        onehot = (owner_ids[:, None] == leaf_ids[None, :]).astype(jnp.int32)
        before = jnp.cumsum(onehot, axis=0) - onehot
        slot_in = jnp.sum(before * onehot, axis=1)
        return (owner_ids * capacity + slot_in, targets)

    forward_out = []
    kept_index = []
    for level in range(levels):
        block = accum[level * block_rows : (level + 1) * block_rows].reshape(
            per_level, grid_rows, columns
        )
        block_bf = block.astype(jnp.bfloat16)
        solved = apply_inverse(fwd_inv[level], block_bf)
        forward_out.append(solved)
        if level < levels - 1:
            lowered = solved.astype(jnp.bfloat16)

            def forward_term(offset, length, lower_cols=upd_t[level], lowered=lowered):
                return jnp.einsum(
                    "kwr,kwn->rkn", lower_cols, lowered, preferred_element_type=jnp.float32
                )

            summed = grid_reduce(forward_term, group_rows)
            routed = summed.reshape(group_rows * per_level, columns)
            slot_pos, targets = placement(level)
            outgoing = jnp.zeros((owners * capacity, columns), jnp.float32).at[slot_pos].set(routed)
            outgoing_index = jnp.zeros((owners * capacity,), jnp.int32).at[slot_pos].set(targets)
            incoming, incoming_index = (
                lax.all_to_all(
                    outgoing.reshape(owners, capacity, columns).astype(jnp.bfloat16),
                    "leaf",
                    split_axis=0,
                    concat_axis=0,
                    tiled=True,
                ).astype(jnp.float32),
                lax.all_to_all(
                    outgoing_index.reshape(owners, capacity),
                    "leaf",
                    split_axis=0,
                    concat_axis=0,
                    tiled=True,
                ),
            )
            accum = accum.at[incoming_index.reshape(-1)].add(-incoming.reshape(-1, columns))
            kept_index.append(incoming_index)
    solution = jnp.zeros((levels * block_rows, columns), jnp.bfloat16)
    for level in reversed(range(levels)):
        reduced = forward_out[level]
        if level < levels - 1:
            slot_pos, targets = placement(level)
            asking = (
                jnp.zeros((owners * capacity,), jnp.int32)
                .at[slot_pos]
                .set(targets)
                .reshape(owners, capacity)
            )

            def answer(asked, solution=solution):
                found = solution[asked.reshape(-1)].reshape(asked.shape[0], asked.shape[1], columns)
                return send_back(found)

            returned = answer(
                lax.all_to_all(asking, "leaf", split_axis=0, concat_axis=0, tiled=True)
            )
            pulled = returned.reshape(owners * capacity, columns)[slot_pos].reshape(
                group_rows, per_level, columns
            )

            def backward_term(offset, length, upper_rows=bwd_t[level], pulled=pulled):
                return jnp.einsum(
                    "kjw,jkn->wkn", upper_rows, pulled, preferred_element_type=jnp.float32
                )

            upper_sum = grid_reduce(backward_term, grid_rows)
            reduced = reduced - jnp.swapaxes(upper_sum, 0, 1)
        result = apply_inverse(bwd_inv[level], reduced.astype(jnp.bfloat16))
        solution = solution.at[level * block_rows : (level + 1) * block_rows].set(
            result.astype(jnp.bfloat16).reshape(block_rows, columns)
        )
    return solution.reshape(levels, per_level, grid_rows, columns)


def solution(mesh):
    placed = (
        P(None, "leaf", "grid", None),
        P(None, "leaf", "grid", None),
        P(None, "leaf", "grid", None),
        P(None, "leaf", "grid", None),
        P(None, "leaf", "grid", None),
        P(None, "leaf", "grid", None, None),
        P(None, "leaf", "grid", None),
    )
    return jax.shard_map(
        local, mesh=mesh, in_specs=placed, out_specs=P(None, "leaf", "grid", None), check_vma=False
    )
```

profile of v0, /device:TPU:32, one launch (start us, length us, event | category | flops | bytes accessed | tf_op | source)
XLA Modules:
  0.0 601.0 jit_solution(17086478699634533320)
XLA Ops:
  7.4 12.6 %all-gather = bf16[1,2,256,256]{3,2,1,0:T(8,128)(2,1)S(1)} all-gather(bf16[1,2,64,256]{3,2,1,0:T(8,128)(2,1)S(1)} %slice-done), channel_id=2, replica_groups=mesh['leaf'=64,'grid'=4] {'grid'}, dimensions={2}, use_global_device_ids=true | all-gather | bytes 327680 | tf_op jit(solution)/shard_map/all_gather | solution.py:11
  33.2 11.8 %all-to-all-start = ((s32[64,1,10]{2,1,0:T(1,128)}), s32[64,1,10]{2,1,0:T(1,128)S(1)}, u32[]{:S(2)}, u32[]{:S(2)}) async-start(s32[64,1,10]{2,1,0:T(1,128)} %bitcast.8), calls=%async_computation | async-start | bytes 65536 | tf_op jit(solution)/shard_map/all_to_all | solution.py:76
  64.8 15.5 %all-to-all-done.1 = bf16[64,10,256]{2,1,0:T(8,128)(2,1)S(1)} async-done(((bf16[64,10,256]{2,1,0:T(8,128)(2,1)}), bf16[64,10,256]{2,1,0:T(8,128)(2,1)S(1)}, u32[]{:S(2)}, u32[]{:S(2)}) %all-to-all-start.1) | async-done | bytes 327712 | tf_op jit(solution)/shard_map/all_to_all | solution.py:69
  86.9 12.3 %all_gather.31 = bf16[2,256,256]{2,1,0:T(8,128)(2,1)S(1)} all-gather(bf16[2,64,256]{2,1,0:T(8,128)(2,1)S(1)} %bitcast.266), channel_id=1, replica_groups=mesh['leaf'=64,'grid'=4] {'grid'}, dimensions={1}, use_global_device_ids=true | all-gather | bytes 327680 | tf_op jit(solution)/shard_map/all_gather | solution.py:11
  110.7 11.1 %reduce-scatter.27.cloned.1.call-done = bf16[128,512]{1,0:T(8,128)(2,1)} async-done(((bf16[512,512]{1,0:T(8,128)(2,1)}), bf16[128,512]{1,0:T(8,128)(2,1)}) %reduce-scatter.27.cloned.1.call-update) | async-done | bytes 131088
  125.7 10.6 %all-to-all-start.3 = ((bf16[64,10,256]{2,1,0:T(8,128)(2,1)}), bf16[64,10,256]{2,1,0:T(8,128)(2,1)S(1)}, u32[]{:S(2)}, u32[]{:S(2)}) async-start(bf16[64,10,256]{2,1,0:T(8,128)(2,1)} %convert_element_type.221), calls=%async_computation.3 | async-start | bytes 1048576 | tf_op jit(solution)/shard_map/all_to_all | solution.py:69
  137.2 16.1 %all-to-all-done.3 = bf16[64,10,256]{2,1,0:T(8,128)(2,1)S(1)} async-done(((bf16[64,10,256]{2,1,0:T(8,128)(2,1)}), bf16[64,10,256]{2,1,0:T(8,128)(2,1)S(1)}, u32[]{:S(2)}, u32[]{:S(2)}) %all-to-all-start.3) | async-done | bytes 327712 | tf_op jit(solution)/shard_map/all_to_all | solution.py:69
  160.0 12.3 %all_gather.32 = bf16[2,256,256]{2,1,0:T(8,128)(2,1)S(1)} all-gather(bf16[2,64,256]{2,1,0:T(8,128)(2,1)S(1)} %bitcast.267), channel_id=1, replica_groups=mesh['leaf'=64,'grid'=4] {'grid'}, dimensions={1}, use_global_device_ids=true | all-gather | bytes 327680 | tf_op jit(solution)/shard_map/all_gather | solution.py:11
  183.6 11.3 %reduce-scatter.29.cloned.1.call-done = bf16[128,512]{1,0:T(8,128)(2,1)} async-done(((bf16[512,512]{1,0:T(8,128)(2,1)}), bf16[128,512]{1,0:T(8,128)(2,1)}) %reduce-scatter.29.cloned.1.call-update) | async-done | bytes 131088
  198.8 10.6 %all-to-all-start.5 = ((bf16[64,10,256]{2,1,0:T(8,128)(2,1)}), bf16[64,10,256]{2,1,0:T(8,128)(2,1)S(1)}, u32[]{:S(2)}, u32[]{:S(2)}) async-start(bf16[64,10,256]{2,1,0:T(8,128)(2,1)} %convert_element_type.230), calls=%async_computation.5 | async-start | bytes 1048576 | tf_op jit(solution)/shard_map/all_to_all | solution.py:69
  210.7 15.7 %all-to-all-done.5 = bf16[64,10,256]{2,1,0:T(8,128)(2,1)S(1)} async-done(((bf16[64,10,256]{2,1,0:T(8,128)(2,1)}), bf16[64,10,256]{2,1,0:T(8,128)(2,1)S(1)}, u32[]{:S(2)}, u32[]{:S(2)}) %all-to-all-start.5) | async-done | bytes 327712 | tf_op jit(solution)/shard_map/all_to_all | solution.py:69
  233.0 12.3 %all_gather.33 = bf16[2,256,256]{2,1,0:T(8,128)(2,1)S(1)} all-gather(bf16[2,64,256]{2,1,0:T(8,128)(2,1)S(1)} %bitcast.268), channel_id=1, replica_groups=mesh['leaf'=64,'grid'=4] {'grid'}, dimensions={1}, use_global_device_ids=true | all-gather | bytes 327680 | tf_op jit(solution)/shard_map/all_gather | solution.py:11
  256.6 11.3 %reduce-scatter.31.cloned.1.call-done = bf16[128,512]{1,0:T(8,128)(2,1)} async-done(((bf16[512,512]{1,0:T(8,128)(2,1)}), bf16[128,512]{1,0:T(8,128)(2,1)}) %reduce-scatter.31.cloned.1.call-update) | async-done | bytes 131088
  271.8 10.6 %all-to-all-start.7 = ((bf16[64,10,256]{2,1,0:T(8,128)(2,1)}), bf16[64,10,256]{2,1,0:T(8,128)(2,1)S(1)}, u32[]{:S(2)}, u32[]{:S(2)}) async-start(bf16[64,10,256]{2,1,0:T(8,128)(2,1)} %convert_element_type.239), calls=%async_computation.7 | async-start | bytes 1048576 | tf_op jit(solution)/shard_map/all_to_all | solution.py:69
  283.3 16.2 %all-to-all-done.7 = bf16[64,10,256]{2,1,0:T(8,128)(2,1)S(1)} async-done(((bf16[64,10,256]{2,1,0:T(8,128)(2,1)}), bf16[64,10,256]{2,1,0:T(8,128)(2,1)S(1)}, u32[]{:S(2)}, u32[]{:S(2)}) %all-to-all-start.7) | async-done | bytes 327712 | tf_op jit(solution)/shard_map/all_to_all | solution.py:69
  306.1 12.5 %all_gather.34 = bf16[2,256,256]{2,1,0:T(8,128)(2,1)S(1)} all-gather(bf16[2,64,256]{2,1,0:T(8,128)(2,1)S(1)} %bitcast.265), channel_id=1, replica_groups=mesh['leaf'=64,'grid'=4] {'grid'}, dimensions={1}, use_global_device_ids=true | all-gather | bytes 327680 | tf_op jit(solution)/shard_map/all_gather | solution.py:11
  319.6 12.3 %all_gather.35 = bf16[2,256,256]{2,1,0:T(8,128)(2,1)S(1)} all-gather(bf16[2,64,256]{2,1,0:T(8,128)(2,1)S(1)} %fusion.4), channel_id=1, replica_groups=mesh['leaf'=64,'grid'=4] {'grid'}, dimensions={1}, use_global_device_ids=true | all-gather | bytes 327680 | tf_op jit(solution)/shard_map/all_gather | solution.py:11
  342.8 17.0 %all-to-all-done.8 = bf16[64,10,256]{2,1,0:T(8,128)(2,1)S(1)} async-done(((bf16[64,10,256]{2,1,0:T(8,128)(2,1)}), bf16[64,10,256]{2,1,0:T(8,128)(2,1)S(1)}, u32[]{:S(2)}, u32[]{:S(2)}) %all-to-all-start.8) | async-done | bytes 327712 | tf_op jit(solution)/shard_map/all_to_all | solution.py:26
  362.2 19.3 %reduce-scatter.17.cloned.1.call-done = bf16[64,2,256]{2,0,1:T(8,128)(2,1)} async-done(((bf16[256,2,256]{2,0,1:T(8,128)(2,1)}), bf16[64,2,256]{2,0,1:T(8,128)(2,1)}) %reduce-scatter.17.cloned.1.call-update) | async-done | bytes 65552 | tf_op jit(solution)/shard_map/reduce_scatter | solution.py:17
  382.3 12.3 %all_gather.36 = bf16[2,256,256]{2,1,0:T(8,128)(2,1)S(1)} all-gather(bf16[2,64,256]{2,1,0:T(8,128)(2,1)S(1)} %fusion.21), channel_id=1, replica_groups=mesh['leaf'=64,'grid'=4] {'grid'}, dimensions={1}, use_global_device_ids=true | all-gather | bytes 327680 | tf_op jit(solution)/shard_map/all_gather | solution.py:11
  398.4 10.5 %all-to-all-start.9 = ((bf16[64,10,256]{2,1,0:T(8,128)(2,1)}), bf16[64,10,256]{2,1,0:T(8,128)(2,1)S(1)}, u32[]{:S(2)}, u32[]{:S(2)}) async-start(bf16[64,10,256]{2,1,0:T(8,128)(2,1)} %reshape.585), calls=%async_computation.10 | async-start | bytes 1048576 | tf_op jit(solution)/shard_map/all_to_all | solution.py:26
  409.0 17.0 %all-to-all-done.9 = bf16[64,10,256]{2,1,0:T(8,128)(2,1)S(1)} async-done(((bf16[64,10,256]{2,1,0:T(8,128)(2,1)}), bf16[64,10,256]{2,1,0:T(8,128)(2,1)S(1)}, u32[]{:S(2)}, u32[]{:S(2)}) %all-to-all-start.9) | async-done | bytes 327712 | tf_op jit(solution)/shard_map/all_to_all | solution.py:26
  428.4 19.3 %reduce-scatter.19.cloned.1.call-done = bf16[64,2,256]{2,0,1:T(8,128)(2,1)} async-done(((bf16[256,2,256]{2,0,1:T(8,128)(2,1)}), bf16[64,2,256]{2,0,1:T(8,128)(2,1)}) %reduce-scatter.19.cloned.1.call-update) | async-done | bytes 65552 | tf_op jit(solution)/shard_map/reduce_scatter | solution.py:17
  448.5 12.3 %all_gather.37 = bf16[2,256,256]{2,1,0:T(8,128)(2,1)S(1)} all-gather(bf16[2,64,256]{2,1,0:T(8,128)(2,1)S(1)} %fusion.19), channel_id=1, replica_groups=mesh['leaf'=64,'grid'=4] {'grid'}, dimensions={1}, use_global_device_ids=true | all-gather | bytes 327680 | tf_op jit(solution)/shard_map/all_gather | solution.py:11
  464.6 10.5 %all-to-all-start.10 = ((bf16[64,10,256]{2,1,0:T(8,128)(2,1)}), bf16[64,10,256]{2,1,0:T(8,128)(2,1)S(1)}, u32[]{:S(2)}, u32[]{:S(2)}) async-start(bf16[64,10,256]{2,1,0:T(8,128)(2,1)} %reshape.589), calls=%async_computation.12 | async-start | bytes 1048576 | tf_op jit(solution)/shard_map/all_to_all | solution.py:26
  475.2 17.0 %all-to-all-done.10 = bf16[64,10,256]{2,1,0:T(8,128)(2,1)S(1)} async-done(((bf16[64,10,256]{2,1,0:T(8,128)(2,1)}), bf16[64,10,256]{2,1,0:T(8,128)(2,1)S(1)}, u32[]{:S(2)}, u32[]{:S(2)}) %all-to-all-start.10) | async-done | bytes 327712 | tf_op jit(solution)/shard_map/all_to_all | solution.py:26
  494.5 19.3 %reduce-scatter.21.cloned.1.call-done = bf16[64,2,256]{2,0,1:T(8,128)(2,1)} async-done(((bf16[256,2,256]{2,0,1:T(8,128)(2,1)}), bf16[64,2,256]{2,0,1:T(8,128)(2,1)}) %reduce-scatter.21.cloned.1.call-update) | async-done | bytes 65552 | tf_op jit(solution)/shard_map/reduce_scatter | solution.py:17
  514.7 12.3 %all_gather.38 = bf16[2,256,256]{2,1,0:T(8,128)(2,1)S(1)} all-gather(bf16[2,64,256]{2,1,0:T(8,128)(2,1)S(1)} %fusion.17), channel_id=1, replica_groups=mesh['leaf'=64,'grid'=4] {'grid'}, dimensions={1}, use_global_device_ids=true | all-gather | bytes 327680 | tf_op jit(solution)/shard_map/all_gather | solution.py:11
  530.8 10.5 %all-to-all-start.11 = ((bf16[64,10,256]{2,1,0:T(8,128)(2,1)}), bf16[64,10,256]{2,1,0:T(8,128)(2,1)S(1)}, u32[]{:S(2)}, u32[]{:S(2)}) async-start(bf16[64,10,256]{2,1,0:T(8,128)(2,1)} %reshape.593), calls=%async_computation.14 | async-start | bytes 1048576 | tf_op jit(solution)/shard_map/all_to_all | solution.py:26
  541.3 17.0 %all-to-all-done.11 = bf16[64,10,256]{2,1,0:T(8,128)(2,1)S(1)} async-done(((bf16[64,10,256]{2,1,0:T(8,128)(2,1)}), bf16[64,10,256]{2,1,0:T(8,128)(2,1)S(1)}, u32[]{:S(2)}, u32[]{:S(2)}) %all-to-all-start.11) | async-done | bytes 327712 | tf_op jit(solution)/shard_map/all_to_all | solution.py:26
  560.7 19.3 %reduce-scatter.23.cloned.1.call-done = bf16[64,2,256]{2,0,1:T(8,128)(2,1)} async-done(((bf16[256,2,256]{2,0,1:T(8,128)(2,1)}), bf16[64,2,256]{2,0,1:T(8,128)(2,1)}) %reduce-scatter.23.cloned.1.call-update) | async-done | bytes 65552 | tf_op jit(solution)/shard_map/reduce_scatter | solution.py:17
  580.8 12.3 %all_gather.39 = bf16[2,256,256]{2,1,0:T(8,128)(2,1)S(1)} all-gather(bf16[2,64,256]{2,1,0:T(8,128)(2,1)S(1)} %fusion.15), channel_id=1, replica_groups=mesh['leaf'=64,'grid'=4] {'grid'}, dimensions={1}, use_global_device_ids=true | all-gather | bytes 327680 | tf_op jit(solution)/shard_map/all_gather | solution.py:11
  (202 shorter events, 145.7 us)
Async XLA Ops:
  6.5 0.8 slice-start
  6.5 14.4 %copy-start.1 = (bf16[4,2,64,512]{3,2,1,0:T(8,128)(2,1)S(1)}, bf16[4,2,64,512]{3,2,1,0:T(8,128)(2,1)}, u32[]{:S(2)}) copy-start(bf16[4,2,64,512]{3,2,1,0:T(8,128)(2,1)} %param.20) | copy-start | bytes 1572868
  6.5 42.2 %reduce-scatter.25.cloned.1.call-start = ((), (), s32[]{:S(2)}) async-start(), calls=%async_computation.24 | async-start | bytes 655360
  22.3 0.7 copy-start.5
  27.5 0.7 slice-start.1
  28.2 0.6 slice-start.2
  29.0 0.7 slice-start.3
  29.8 0.6 slice-start.4
  30.4 0.7 copy-start.10
  33.2 20.3 %all-to-all-start = ((s32[64,1,10]{2,1,0:T(1,128)}), s32[64,1,10]{2,1,0:T(1,128)S(1)}, u32[]{:S(2)}, u32[]{:S(2)}) async-start(s32[64,1,10]{2,1,0:T(1,128)} %bitcast.8), calls=%async_computation | async-start | bytes 65536 | tf_op jit(solution)/shard_map/all_to_all | solution.py:76
  52.6 10.7 %copy-start.3 = (bf16[5,2,64,256]{3,2,1,0:T(8,128)(2,1)S(1)}, bf16[5,2,64,256]{3,2,1,0:T(8,128)(2,1)}, u32[]{:S(2)}) copy-start(bf16[5,2,64,256]{3,2,1,0:T(8,128)(2,1)} %param.17) | copy-start | bytes 983044
  53.5 26.8 %all-to-all-start.1 = ((bf16[64,10,256]{2,1,0:T(8,128)(2,1)}), bf16[64,10,256]{2,1,0:T(8,128)(2,1)S(1)}, u32[]{:S(2)}, u32[]{:S(2)}) async-start(bf16[64,10,256]{2,1,0:T(8,128)(2,1)} %convert_element_type.212), calls=%async_computation.1 | async-start | bytes 1048576 | tf_op jit(solution)/shard_map/all_to_all | solution.py:69
  63.3 58.5 %reduce-scatter.27.cloned.1.call-start = ((), (), s32[]{:S(2)}) async-start(), calls=%async_computation.25 | async-start | bytes 655360
  103.8 21.9 %all-to-all-start.2 = ((s32[64,1,10]{2,1,0:T(1,128)}), s32[64,1,10]{2,1,0:T(1,128)S(1)}, u32[]{:S(2)}, u32[]{:S(2)}) async-start(s32[64,1,10]{2,1,0:T(1,128)} %bitcast.20), calls=%async_computation.2 | async-start | bytes 65536 | tf_op jit(solution)/shard_map/all_to_all | solution.py:76
  125.7 27.7 %all-to-all-start.3 = ((bf16[64,10,256]{2,1,0:T(8,128)(2,1)}), bf16[64,10,256]{2,1,0:T(8,128)(2,1)S(1)}, u32[]{:S(2)}, u32[]{:S(2)}) async-start(bf16[64,10,256]{2,1,0:T(8,128)(2,1)} %convert_element_type.221), calls=%async_computation.3 | async-start | bytes 1048576 | tf_op jit(solution)/shard_map/all_to_all | solution.py:69
  136.3 58.6 %reduce-scatter.29.cloned.1.call-start = ((), (), s32[]{:S(2)}) async-start(), calls=%async_computation.26 | async-start | bytes 655360
  176.8 21.9 %all-to-all-start.4 = ((s32[64,1,10]{2,1,0:T(1,128)}), s32[64,1,10]{2,1,0:T(1,128)S(1)}, u32[]{:S(2)}, u32[]{:S(2)}) async-start(s32[64,1,10]{2,1,0:T(1,128)} %bitcast.33), calls=%async_computation.4 | async-start | bytes 65536 | tf_op jit(solution)/shard_map/all_to_all | solution.py:76
  198.8 27.7 %all-to-all-start.5 = ((bf16[64,10,256]{2,1,0:T(8,128)(2,1)}), bf16[64,10,256]{2,1,0:T(8,128)(2,1)S(1)}, u32[]{:S(2)}, u32[]{:S(2)}) async-start(bf16[64,10,256]{2,1,0:T(8,128)(2,1)} %convert_element_type.230), calls=%async_computation.5 | async-start | bytes 1048576 | tf_op jit(solution)/shard_map/all_to_all | solution.py:69
  209.4 58.6 %reduce-scatter.31.cloned.1.call-start = ((), (), s32[]{:S(2)}) async-start(), calls=%async_computation.27 | async-start | bytes 655360
  249.9 22.0 %all-to-all-start.6 = ((s32[64,1,10]{2,1,0:T(1,128)}), s32[64,1,10]{2,1,0:T(1,128)S(1)}, u32[]{:S(2)}, u32[]{:S(2)}) async-start(s32[64,1,10]{2,1,0:T(1,128)} %bitcast.46), calls=%async_computation.6 | async-start | bytes 65536 | tf_op jit(solution)/shard_map/all_to_all | solution.py:76
  271.8 27.6 %all-to-all-start.7 = ((bf16[64,10,256]{2,1,0:T(8,128)(2,1)}), bf16[64,10,256]{2,1,0:T(8,128)(2,1)S(1)}, u32[]{:S(2)}, u32[]{:S(2)}) async-start(bf16[64,10,256]{2,1,0:T(8,128)(2,1)} %convert_element_type.239), calls=%async_computation.7 | async-start | bytes 1048576 | tf_op jit(solution)/shard_map/all_to_all | solution.py:69
  318.6 13.3 %copy-start.4 = (bf16[5,2,64,256]{3,2,1,0:T(8,128)(2,1)S(1)}, bf16[5,2,64,256]{3,2,1,0:T(8,128)(2,1)}, u32[]{:S(2)}) copy-start(bf16[5,2,64,256]{3,2,1,0:T(8,128)(2,1)} %param.19) | copy-start | bytes 983044
  335.8 24.0 %all-to-all-start.8 = ((bf16[64,10,256]{2,1,0:T(8,128)(2,1)}), bf16[64,10,256]{2,1,0:T(8,128)(2,1)S(1)}, u32[]{:S(2)}, u32[]{:S(2)}) async-start(bf16[64,10,256]{2,1,0:T(8,128)(2,1)} %reshape.581), calls=%async_computation.8 | async-start | bytes 1048576 | tf_op jit(solution)/shard_map/all_to_all | solution.py:26
  342.7 38.7 %reduce-scatter.17.cloned.1.call-start = ((), (), s32[]{:S(2)}) async-start(), calls=%async_computation.20 | async-start | bytes 327680 | tf_op jit(solution)/shard_map/reduce_scatter | solution.py:17
  359.9 1.2 copy-start.2
  398.4 27.6 %all-to-all-start.9 = ((bf16[64,10,256]{2,1,0:T(8,128)(2,1)}), bf16[64,10,256]{2,1,0:T(8,128)(2,1)S(1)}, u32[]{:S(2)}, u32[]{:S(2)}) async-start(bf16[64,10,256]{2,1,0:T(8,128)(2,1)} %reshape.585), calls=%async_computation.10 | async-start | bytes 1048576 | tf_op jit(solution)/shard_map/all_to_all | solution.py:26
  408.9 38.7 %reduce-scatter.19.cloned.1.call-start = ((), (), s32[]{:S(2)}) async-start(), calls=%async_computation.21 | async-start | bytes 327680 | tf_op jit(solution)/shard_map/reduce_scatter | solution.py:17
  464.6 27.5 %all-to-all-start.10 = ((bf16[64,10,256]{2,1,0:T(8,128)(2,1)}), bf16[64,10,256]{2,1,0:T(8,128)(2,1)S(1)}, u32[]{:S(2)}, u32[]{:S(2)}) async-start(bf16[64,10,256]{2,1,0:T(8,128)(2,1)} %reshape.589), calls=%async_computation.12 | async-start | bytes 1048576 | tf_op jit(solution)/shard_map/all_to_all | solution.py:26
  475.1 38.7 %reduce-scatter.21.cloned.1.call-start = ((), (), s32[]{:S(2)}) async-start(), calls=%async_computation.22 | async-start | bytes 327680 | tf_op jit(solution)/shard_map/reduce_scatter | solution.py:17
  530.8 27.5 %all-to-all-start.11 = ((bf16[64,10,256]{2,1,0:T(8,128)(2,1)}), bf16[64,10,256]{2,1,0:T(8,128)(2,1)S(1)}, u32[]{:S(2)}, u32[]{:S(2)}) async-start(bf16[64,10,256]{2,1,0:T(8,128)(2,1)} %reshape.593), calls=%async_computation.14 | async-start | bytes 1048576 | tf_op jit(solution)/shard_map/all_to_all | solution.py:26
  541.3 38.7 %reduce-scatter.23.cloned.1.call-start = ((), (), s32[]{:S(2)}) async-start(), calls=%async_computation.23 | async-start | bytes 327680 | tf_op jit(solution)/shard_map/reduce_scatter | solution.py:17
  593.3 0.7 copy-start
  (4 other events, 2.3 us)
Sparse Core Ops, SparseCore 0:
  22.5 26.2 reduce-scatter.24
  101.7 20.0 reduce-scatter.26
  174.8 20.0 reduce-scatter.28
  247.8 20.0 reduce-scatter.30
  362.3 19.1 reduce-scatter.16
  428.5 19.1 reduce-scatter.18
  494.6 19.1 reduce-scatter.20
  560.8 19.1 reduce-scatter.22
where the time goes:
time: 611 us; the launch traced here: 601 us
  waiting for transfers between devices  247 us (40%)
  blocking collectives  123 us (20%)
  starting transfers between devices  113 us (18%)
  local copies, waits for them, and re-layouts  56.7 us (9%)
  other arithmetic  35.3 us (6%)
  between operations  14.5 us (2%)
  matrix products  11.2 us (2%)
    all_gather x10, blocking collectives, apply_inverse(): lax.all_gather(block_bf, 'grid', axis=1, tiled=True)  123 us
    reduce_scatter x4, waiting for transfers between devices, grid_reduce(): lax.psum_scatter(term_fn(jnp.int32(0), kept_rows * lax.axis_size('grid'))...  77.2 us
    all_to_all x4, waiting for transfers between devices, send_back(): lax.all_to_all(solved_rows, 'leaf', split_axis=0, concat_axis=0, tiled=True)  68 us
    all_to_all x4, waiting for transfers between devices, local(): lax.all_to_all(outgoing.reshape(owners, capacity, columns).astype(jnp.bfl...  63.6 us
    all_to_all x4, starting transfers between devices, local(): lax.all_to_all(outgoing.reshape(owners, capacity, columns).astype(jnp.bfl...  41.5 us
    all_to_all x4, starting transfers between devices, send_back(): lax.all_to_all(solved_rows, 'leaf', split_axis=0, concat_axis=0, tiled=True)  38.4 us
    unnamed x12, waiting for transfers between devices  37.6 us
    all_to_all x4, starting transfers between devices, local(): lax.all_to_all(outgoing_index.reshape(owners, capacity), 'leaf', split_ax...  32.1 us
  transfers between devices with their start and end apart: 20, of which 17 were waited for; matrix products, arithmetic and copies ran while one was open for 5% of the time, Pallas kernels for 0%

commit v1 on v0

v1 whole, which is shorter than its diff:
```python
import jax
import jax.numpy as jnp
from jax import lax
from jax.experimental import pallas as pl
from jax.experimental.pallas import tpu as pltpu
from jax.sharding import PartitionSpec as P

MESH = pl.DeviceIdType.MESH
BF = jnp.bfloat16
F32 = jnp.float32
LANES = 128


def dot(a, b):
    return jnp.dot(a, b, preferred_element_type=F32)


def dot_t(a, b):
    return lax.dot_general(a, b, (((0,), (0,)), ((), ())), preferred_element_type=F32)


def solve_kernel(
    sizes,
    rhs,
    fwd_inv,
    bwd_inv,
    upd,
    bwd,
    pos_r,
    pos_c,
    idx_r,
    idx_c,
    out,
    finv,
    binv,
    ucol,
    blk,
    low,
    acc,
    const,
    sol,
    sbuf,
    rbuf,
    rs_s,
    rs_r,
    pm,
    pt,
    sm,
    gm,
    fs,
    fr,
    us,
    ur,
    bs,
    br,
    ag_s,
    ag_r,
    aa_s,
    aa_r,
    rd_s,
    rd_r,
):
    levels, per, rows, group_rows, owners, groups, cap, halves = sizes
    sends = levels - 1
    width = rows * groups
    block = per * rows
    slots = owners * cap
    routed = per * group_rows
    me = lax.axis_index("leaf")
    gx = lax.axis_index("grid")
    my_rows = pl.ds(pl.multiple_of(gx * rows, rows), rows)
    others = owners - 1

    def peer(step):
        return lax.rem(gx + step, groups)

    def remote(src, dst, send, recv, leaf, grid):
        return pltpu.make_async_remote_copy(
            src_ref=src,
            dst_ref=dst,
            send_sem=send,
            recv_sem=recv,
            device_id=(leaf, grid),
            device_id_type=MESH,
        )

    barrier = pltpu.get_barrier_semaphore()

    def greet(i, c):
        pl.semaphore_signal(
            barrier, inc=1, device_id=(lax.rem(me + i, owners), gx), device_id_type=MESH
        )
        return c

    lax.fori_loop(1, owners, greet, 0)
    for step in range(1, groups):
        pl.semaphore_signal(barrier, inc=1, device_id=(me, peer(step)), device_id_type=MESH)
    pl.semaphore_wait(barrier, others + groups - 1)

    def part(ref, count):
        return ref.at[:, pl.ds(0, count), :]

    def matrix(level, ref, mine, send, recv):
        for step in range(1, groups):
            remote(
                mine.at[level],
                ref.at[level, :, my_rows, :],
                send.at[level],
                recv.at[level],
                me,
                peer(step),
            ).start()

    def matrix_sync(level, ref, send, recv, sent):
        view = part(ref.at[level], width - rows)
        copy = remote(view, view, send.at[level], recv.at[level], me, peer(1))
        copy.wait_send() if sent else copy.wait_recv()

    def columns(level):
        for step in range(1, groups):
            to = peer(step)
            remote(
                upd.at[level, :, :, pl.ds(pl.multiple_of(to * group_rows, group_rows), group_rows)],
                ucol.at[level, :, my_rows, :],
                us.at[level],
                ur.at[level],
                me,
                to,
            ).start()

    def gather(level, h):
        view = blk.at[level, h, :, my_rows, :]
        for step in range(1, groups):
            remote(view, view, ag_s.at[level, h], ag_r.at[level, h], me, peer(step)).start()

    def gather_sync(level, h, sent):
        view = part(blk.at[level, h], width - rows)
        copy = remote(view, view, ag_s.at[level, h], ag_r.at[level, h], me, peer(1))
        copy.wait_send() if sent else copy.wait_recv()

    def exchange(phase, h):
        def body(i, c):
            to = lax.rem(me + i, owners)
            remote(
                sbuf.at[phase, h, to],
                rbuf.at[phase, h, me],
                aa_s.at[phase, h],
                aa_r.at[phase, h],
                to,
                gx,
            ).start()
            return c

        lax.fori_loop(1, owners, body, 0)
        rbuf[phase, h, me] = sbuf[phase, h, me]

    def exchange_sync(phase, h, sent):
        view = (sbuf if sent else rbuf).at[phase, h, pl.ds(0, others)]
        to = lax.rem(me + 1, owners)
        copy = remote(view, view, aa_s.at[phase, h], aa_r.at[phase, h], to, gx)
        copy.wait_send() if sent else copy.wait_recv()

    def reduce_start(level, h):
        for step in range(1, groups):
            to = peer(step)
            remote(
                rs_s.at[level, h, :, pl.ds(pl.multiple_of(to * rows, rows), rows), :],
                rs_r.at[level, h, gx],
                rd_s.at[level, h],
                rd_r.at[level, h],
                me,
                to,
            ).start()

    def reduce_sync(level, h, sent):
        view = rs_r.at[level, h, pl.ds(0, groups - 1)]
        copy = remote(view, view, rd_s.at[level, h], rd_r.at[level, h], me, peer(1))
        copy.wait_send() if sent else copy.wait_recv()

    def hot(mask):
        return jnp.where(mask, 1.0, 0.0).astype(BF)

    def build_p(level):
        for c in range(slots // LANES):
            at = lax.broadcasted_iota(jnp.int32, (LANES, routed), 0) + c * LANES
            pm[level, pl.ds(c * LANES, LANES), :] = hot(at == pos_r[level])

    def build_pt(level):
        for c in range(routed // LANES):
            span = pl.ds(c * LANES, LANES)
            at = lax.broadcasted_iota(jnp.int32, (LANES, slots), 1)
            pt[level, span, :] = hot(at == pos_c[level, span, :])

    def build_s(level):
        for c in range(sends * block // LANES):
            at = lax.broadcasted_iota(jnp.int32, (LANES, slots), 0) + (c * LANES + block + 1)
            sm[level, pl.ds(c * LANES, LANES), :] = hot(at == idx_r[level])

    def build_g(level):
        for c in range(slots // LANES):
            span = pl.ds(c * LANES, LANES)
            at = lax.broadcasted_iota(jnp.int32, (LANES, sends * block), 1) + (block + 1)
            gm[level, span, :] = hot(at == idx_c[level, span, :])

    def pack(phase, h, value):
        sbuf[phase, h] = value.astype(BF).reshape(owners, cap // 2, 2, LANES)

    def unpack(phase, h):
        return rbuf[phase, h].reshape(slots, LANES)

    for h in range(halves):
        blk[0, h, :, my_rows, :] = rhs[0, :, :, h * LANES : (h + 1) * LANES]
        gather(0, h)
    matrix(0, finv, fwd_inv, fs, fr)
    columns(0)
    my_columns = pl.ds(pl.multiple_of(gx * group_rows, group_rows), group_rows)
    for level in range(levels):
        finv[level, :, my_rows, :] = fwd_inv[level]
        if level < sends:
            binv[level, :, my_rows, :] = bwd_inv[level]
            ucol[level, :, my_rows, :] = upd[level, :, :, my_columns]
        if level > 0:
            for h in range(halves):
                acc[level, h] = (
                    rhs[level, :, :, h * LANES : (h + 1) * LANES].astype(F32).reshape(block, LANES)
                )
    for level in range(sends):
        build_p(level)

    def lower(level, h):
        matrix_waited = []
        for k in range(per):
            solved = dot(finv[level, k], blk[level, h, k])
            low[h, k] = solved.astype(BF)
            matrix_waited.append(low[h, k])
        return matrix_waited

    def forward(level, c):
        matrix_sync(level, finv, fs, fr, False)
        view = part(ucol.at[level], width - rows)
        remote(view, view, us.at[level], ur.at[level], me, peer(1)).wait_recv()
        for h in range(halves):
            gather_sync(level, h, False)
            lowered = lower(level, h)
            summed = [dot_t(ucol[level, k], lowered[k]).astype(BF) for k in range(per)]
            packed = dot(pm[level], jnp.concatenate(summed, axis=0))
            pack(level, h, packed)
            exchange(level, h)
        matrix(level + 1, finv, fwd_inv, fs, fr)

        @pl.when(level < sends - 1)
        def _():
            columns(level + 1)

        @pl.when(level == sends - 1)
        def _():
            matrix(sends - 1, binv, bwd_inv, bs, br)

        build_s(level)
        build_g(level)
        build_pt(level)
        for h in range(halves):
            for k in range(per):
                const[level, h, k] = dot(bwd_inv[level, k], low[h, k])
        for h in range(halves):
            exchange_sync(level, h, False)
            come = unpack(level, h)
            chosen = sm[level, pl.ds(pl.multiple_of(level * block, block), block), :]
            total = acc[level + 1, h] - dot(chosen, come)
            blk[level + 1, h, :, my_rows, :] = total.astype(BF).reshape(per, rows, LANES)
            gather(level + 1, h)
        for h in range(halves):
            come = unpack(level, h)

            def later(target, c, h=h, come=come):
                span = pl.ds(pl.multiple_of((target - 1) * block, block), block)
                acc[target, h] = acc[target, h] - dot(sm[level, span, :], come)
                return c

            lax.fori_loop(level + 2, levels, later, 0)
        return c

    lax.fori_loop(0, sends, forward, 0)

    def finish(level, h, k, value):
        result = value.astype(BF)
        at = level * block + k * rows
        if not isinstance(at, int):
            at = pl.multiple_of(at, rows)
        sol[h, pl.ds(at, rows), :] = result
        out[level, k, :, h * LANES : (h + 1) * LANES] = result

    sol[...] = jnp.zeros(sol.shape, BF)
    matrix_sync(sends, finv, fs, fr, False)
    for h in range(halves):
        gather_sync(sends, h, False)
        lowered = lower(sends, h)
        for k in range(per):
            finish(sends, h, k, dot(bwd_inv[sends, k], lowered[k]))

    def backward(i, c):
        level = sends - 1 - i
        phase = sends + level
        for h in range(halves):
            answer = dot(gm[level], sol[h, pl.ds(block, sends * block), :])
            pack(phase, h, answer)
            exchange(phase, h)

        @pl.when(level > 0)
        def _():
            matrix(level - 1, binv, bwd_inv, bs, br)

        matrix_sync(level, binv, bs, br, False)
        for h in range(halves):
            exchange_sync(phase, h, False)
            pulled = dot(pt[level], unpack(phase, h)).astype(BF)
            for k in range(per):
                upper = dot_t(bwd[level, k], pulled[k * group_rows : (k + 1) * group_rows])
                rs_s[level, h, k] = dot(binv[level, k], upper.astype(BF)).astype(BF)
            reduce_start(level, h)
        for h in range(halves):
            reduce_sync(level, h, False)
            for k in range(per):
                total = rs_s[level, h, k, my_rows, :].astype(F32)
                for step in range(1, groups):
                    total = total + rs_r[level, h, peer(step), k].astype(F32)
                finish(level, h, k, const[level, h, k] - total)
        return c

    lax.fori_loop(0, sends, backward, 0)

    def drain(level, c):
        matrix_sync(level, finv, fs, fr, True)
        for h in range(halves):
            gather_sync(level, h, True)
        return c

    lax.fori_loop(0, levels, drain, 0)

    def drain_sends(level, c):
        matrix_sync(level, binv, bs, br, True)
        view = part(ucol.at[level], width - rows)
        remote(view, view, us.at[level], ur.at[level], me, peer(1)).wait_send()
        for h in range(halves):
            exchange_sync(level, h, True)
            exchange_sync(level + sends, h, True)
            reduce_sync(level, h, True)
        return c

    lax.fori_loop(0, sends, drain_sends, 0)


def local(rhs, fwd_inv, bwd_inv, upd_t, bwd_t, dest_owner, dest_row):
    levels, per, rows, cols = rhs.shape
    group_rows = bwd_t.shape[2]
    owners = lax.axis_size("leaf")
    groups = lax.axis_size("grid")
    cap = max(2, 8 * per * group_rows // (3 * owners))
    sends = levels - 1
    halves = cols // LANES
    slots = owners * cap
    routed = per * group_rows
    block = per * rows
    width = rows * groups

    def by_supernode(index):
        split = index.reshape(sends, group_rows, per)
        return jnp.swapaxes(split, 1, 2).reshape(sends, routed)

    owner = by_supernode(dest_owner)
    target = by_supernode(dest_row)
    order = jnp.arange(routed, dtype=jnp.int32)
    same = (owner[:, :, None] == owner[:, None, :]) & (order[None, None, :] < order[None, :, None])
    position = owner * cap + jnp.sum(same.astype(jnp.int32), axis=2)
    slot_ids = jnp.arange(slots, dtype=jnp.int32)
    chosen = slot_ids[None, :, None] == position[:, None, :]
    asked = jnp.sum(jnp.where(chosen, target[:, None, :] + 1, 0), axis=2)
    asked = jnp.swapaxes(asked.reshape(sends, owners, cap), 0, 1).reshape(owners, sends * cap)
    told = lax.all_to_all(asked, "leaf", split_axis=0, concat_axis=0, tiled=True)
    told = jnp.swapaxes(told.reshape(owners, sends, cap), 0, 1).reshape(sends, slots)

    dma = pltpu.SemaphoreType.DMA
    vmem = pltpu.VMEM
    sizes = (levels, per, rows, group_rows, owners, groups, cap, halves)

    def body(*refs):
        solve_kernel(sizes, *refs)

    return pl.pallas_call(
        body,
        out_shape=jax.ShapeDtypeStruct(rhs.shape, BF),
        in_specs=[pl.BlockSpec(memory_space=vmem)] * 9,
        out_specs=pl.BlockSpec(memory_space=vmem),
        scratch_shapes=[
            vmem((levels, per, width, width), BF),
            vmem((sends, per, width, width), BF),
            vmem((sends, per, width, group_rows), BF),
            vmem((levels, halves, per, width, LANES), BF),
            vmem((halves, per, width, LANES), BF),
            vmem((levels, halves, block, LANES), F32),
            vmem((sends, halves, per, rows, LANES), F32),
            vmem((halves, levels * block, LANES), BF),
            vmem((2 * sends, halves, owners, cap // 2, 2, LANES), BF),
            vmem((2 * sends, halves, owners, cap // 2, 2, LANES), BF),
            vmem((sends, halves, per, width, LANES), BF),
            vmem((sends, halves, groups, per, rows, LANES), BF),
            vmem((sends, slots, routed), BF),
            vmem((sends, routed, slots), BF),
            vmem((sends, sends * block, slots), BF),
            vmem((sends, slots, sends * block), BF),
            dma((levels,)),
            dma((levels,)),
            dma((sends,)),
            dma((sends,)),
            dma((sends,)),
            dma((sends,)),
            dma((levels, halves)),
            dma((levels, halves)),
            dma((2 * sends, halves)),
            dma((2 * sends, halves)),
            dma((sends, halves)),
            dma((sends, halves)),
        ],
        compiler_params=pltpu.CompilerParams(collective_id=0, has_side_effects=True),
    )(
        rhs,
        fwd_inv,
        bwd_inv,
        upd_t,
        bwd_t,
        position[:, None, :],
        position[:, :, None],
        told[:, None, :],
        told[:, :, None],
    )


def solution(mesh):
    placed = (
        P(None, "leaf", "grid", None),
        P(None, "leaf", "grid", None),
        P(None, "leaf", "grid", None),
        P(None, "leaf", "grid", None),
        P(None, "leaf", "grid", None),
        P(None, "leaf", "grid", None, None),
        P(None, "leaf", "grid", None),
    )
    return jax.shard_map(
        local, mesh=mesh, in_specs=placed, out_specs=P(None, "leaf", "grid", None), check_vma=False
    )
```

time: 611 us -> 168 us (0.27); the launches traced: 601 us -> 168 us
  waiting for transfers between devices: 247 us -> 6.81 us
  Pallas kernels: 0 us -> 140 us
  blocking collectives: 123 us -> 0 us
  starting transfers between devices: 113 us -> 11.8 us
  local copies, waits for them, and re-layouts: 56.7 us -> 7.25 us
  other arithmetic: 35.3 us -> 2.18 us
  between operations: 14.5 us -> 0.08 us
  matrix products: 11.2 us -> 0 us
    pallas_call x0 -> x1, Pallas kernels: none -> 140 us  [local(): pl.pallas_call(body, out_shape=jax.ShapeDtypeStruct(rhs.shape, BF), in_sp...]
    all_to_all x12 -> x1, waiting for transfers between devices: 133 us -> 6.81 us  [local(): lax.all_to_all(asked, 'leaf', split_axis=0, concat_axis=0, tiled=True)]
    all_gather x10 -> x0, blocking collectives: 123 us -> none  [apply_inverse(): lax.all_gather(block_bf, 'grid', axis=1, tiled=True)]
    all_to_all x12 -> x1, starting transfers between devices: 112 us -> 11.8 us  [local(): lax.all_to_all(asked, 'leaf', split_axis=0, concat_axis=0, tiled=True)]
    reduce_scatter x4 -> x0, waiting for transfers between devices: 77.2 us -> none  [grid_reduce(): lax.psum_scatter(term_fn(jnp.int32(0), kept_rows * lax.axis_size('grid'))...]
    unnamed x12 -> x0, waiting for transfers between devices: 37.6 us -> none
    scatter-add x4 -> x0, other arithmetic: 25.3 us -> none  [local(): accum.at[incoming_index.reshape(-1)].add(-incoming.reshape(-1, columns))]
    gather x8 -> x0, local copies, waits for them, and re-layouts: 15.7 us -> none  [the longest x4 11.1 us: answer(): solution[asked.reshape(-1)].reshape(asked.shape[0], asked.shape[1], columns)]
  transfers between devices with their start and end apart: 20 -> 1, of which waited for: 17 -> 1; matrix products, arithmetic and copies ran while one was open for 5% -> 1% of each run, Pallas kernels for 0% -> 0%
where the time goes in v1:
time: 168 us
  Pallas kernels  140 us (83%)
  starting transfers between devices  11.8 us (7%)
  local copies, waits for them, and re-layouts  7.25 us (4%)
  waiting for transfers between devices  6.81 us (4%)
  other arithmetic  2.18 us (1%)
    pallas_call x1, Pallas kernels, local(): pl.pallas_call(body, out_shape=jax.ShapeDtypeStruct(rhs.shape, BF), in_sp...  140 us
    all_to_all x1, starting transfers between devices, local(): lax.all_to_all(asked, 'leaf', split_axis=0, concat_axis=0, tiled=True)  11.8 us
    all_to_all x1, waiting for transfers between devices, local(): lax.all_to_all(asked, 'leaf', split_axis=0, concat_axis=0, tiled=True)  6.81 us
  transfers between devices with their start and end apart: 1, of which 1 were waited for; matrix products, arithmetic and copies ran while one was open for 1% of the time, Pallas kernels for 0%

profile of v1, /device:TPU:32, one launch (start us, length us, event | category | flops | bytes accessed | tf_op | source)
XLA Modules:
  0.0 167.6 jit_solution(11760999038813471849)
XLA Ops:
  0.0 0.7 broadcast_add_fusion
  0.7 0.1 copy.56
  0.9 0.1 copy.57
  0.9 0.8 copy.53
  1.8 0.1 copy.54
  1.9 0.4 convert_reduce_fusion
  2.3 0.4 select_reduce_fusion
  2.7 0.1 reshape.84
  2.9 0.1 copy.58
  3.0 0.7 copy.59
  3.7 11.8 %all-to-all-start = ((s32[64,1,40]{2,1,0:T(1,128)}), s32[64,1,40]{2,1,0:T(1,128)S(1)}, u32[]{:S(2)}, u32[]{:S(2)}) async-start(s32[64,1,40]{2,1,0:T(1,128)} %copy.59), calls=%async_computation | async-start | bytes 65536 | tf_op jit(solution)/shard_map/all_to_all | solution.py:379
  15.5 0.6 reshape_add_fusion.refs_5_
  16.1 1.1 copy.63.refs_6_
  17.2 6.8 %all-to-all-done = s32[64,1,40]{2,1,0:T(1,128)S(1)} async-done(((s32[64,1,40]{2,1,0:T(1,128)}), s32[64,1,40]{2,1,0:T(1,128)S(1)}, u32[]{:S(2)}, u32[]{:S(2)}) %all-to-all-start) | async-done | bytes 10272 | tf_op jit(solution)/shard_map/all_to_all | solution.py:379
  24.0 0.1 copy.60
  24.0 0.1 copy.61
  24.2 0.8 broadcast_in_dim_reshape.11.refs_7_
  24.9 1.4 broadcast_in_dim_reshape.12.refs_8_
  26.4 139.5 %shard_map.73 = bf16[5,2,64,256]{3,2,1,0:T(8,128)(2,1)} custom-call(bf16[5,2,64,256]{3,2,1,0:T(8,128)(2,1)} %refs_0_.1, bf16[5,2,64,256]{3,2,1,0:T(8,128)(2,1)} %refs_1_.1, bf16[5,2,64,256]{3,2,1,0:T(8,128)(2,1)} %refs_2_.1, bf16[4,2,64,512]{3,2,1,0:T(8,128)(2,1)} %refs_3_.1, bf16[4,2,128,256]{3,2,1,0:T(8,128)(2,1)} %refs_4_.1, ...), custom_call_target="tpu_custom_call" | custom-call | tf_op jit(solution)/shard_map/pallas_call | solution.py:389
  165.9 1.7 %copy.67 = bf16[5,2,64,256]{3,2,1,0:T(8,128)(2,1)} copy(bf16[5,2,64,256]{3,2,1,0:T(8,128)(2,1)} %shard_map.73) | data formatting | bytes 655360
  (7 shorter events, 0.1 us)
Async XLA Ops:
  3.7 20.3 %all-to-all-start = ((s32[64,1,40]{2,1,0:T(1,128)}), s32[64,1,40]{2,1,0:T(1,128)S(1)}, u32[]{:S(2)}, u32[]{:S(2)}) async-start(s32[64,1,40]{2,1,0:T(1,128)} %copy.59), calls=%async_computation | async-start | bytes 65536 | tf_op jit(solution)/shard_map/all_to_all | solution.py:379

commit v2 on v1

--- a/solution.py
+++ b/solution.py
@@ -9,6 +9,8 @@
 BF = jnp.bfloat16
 F32 = jnp.float32
 LANES = 128
+RING_Y, RING_Z, CORES = 4, 8, 2
+SLOT_LANES = 16
 
 
 def dot(a, b):
@@ -17,6 +19,10 @@
 
 def dot_t(a, b):
     return lax.dot_general(a, b, (((0,), (0,)), ((), ())), preferred_element_type=F32)
+
+
+def count_out(place, count):
+    return count // 2 + (place + 1) // 2 * (1 - 2 * (place % 2))
 
 
 def solve_kernel(
@@ -26,10 +32,9 @@
     bwd_inv,
     upd,
     bwd,
-    pos_r,
-    pos_c,
-    idx_r,
-    idx_c,
+    own_r,
+    own_c,
+    want_r,
     out,
     finv,
     binv,
@@ -47,6 +52,13 @@
     pt,
     sm,
     gm,
+    told,
+    by_row,
+    by_col,
+    asked,
+    pick,
+    pos_r,
+    pos_c,
     fs,
     fr,
     us,
@@ -59,6 +71,8 @@
     aa_r,
     rd_s,
     rd_r,
+    ix_s,
+    ix_r,
 ):
     levels, per, rows, group_rows, owners, groups, cap, halves = sizes
     sends = levels - 1
@@ -70,9 +84,35 @@
     gx = lax.axis_index("grid")
     my_rows = pl.ds(pl.multiple_of(gx * rows, rows), rows)
     others = owners - 1
+    my_y = lax.div(me, RING_Z * CORES)
+    my_z = lax.rem(lax.div(me, CORES), RING_Z)
+    my_core = lax.rem(me, CORES)
 
     def peer(step):
         return lax.rem(gx + step, groups)
+
+    def outward(place, count):
+        half = lax.div(place + 1, 2)
+        return count // 2 + half * (1 - 2 * lax.rem(place, 2))
+
+    ring = [
+        lax.rem(my_z + count_out(a, RING_Z), RING_Z) * CORES for a in range(RING_Z)
+    ]
+
+    def each_partner(act):
+        def group(j, last):
+            y = lax.rem(my_y + outward(lax.rem(j, RING_Y), RING_Y), RING_Y)
+            core = lax.rem(my_core + 1 - lax.div(j, RING_Y), CORES)
+            base = y * (RING_Z * CORES) + core
+            for a in range(RING_Z - last):
+                act(base + ring[a])
+
+        def body(j, c):
+            group(j, 0)
+            return c
+
+        lax.fori_loop(0, RING_Y * CORES - 1, body, 0)
+        group(jnp.int32(RING_Y * CORES - 1), 1)
 
     def remote(src, dst, send, recv, leaf, grid):
         return pltpu.make_async_remote_copy(
@@ -86,16 +126,12 @@
 
     barrier = pltpu.get_barrier_semaphore()
 
-    def greet(i, c):
-        pl.semaphore_signal(
-            barrier, inc=1, device_id=(lax.rem(me + i, owners), gx), device_id_type=MESH
-        )
-        return c
-
-    lax.fori_loop(1, owners, greet, 0)
+    def greet(to):
+        pl.semaphore_signal(barrier, inc=1, device_id=(to, gx), device_id_type=MESH)
+
+    each_partner(greet)
     for step in range(1, groups):
         pl.semaphore_signal(barrier, inc=1, device_id=(me, peer(step)), device_id_type=MESH)
-    pl.semaphore_wait(barrier, others + groups - 1)
 
     def part(ref, count):
         return ref.at[:, pl.ds(0, count), :]
@@ -139,8 +175,7 @@
         copy.wait_send() if sent else copy.wait_recv()
 
     def exchange(phase, h):
-        def body(i, c):
-            to = lax.rem(me + i, owners)
+        def send(to):
             remote(
                 sbuf.at[phase, h, to],
                 rbuf.at[phase, h, me],
@@ -149,9 +184,8 @@
                 to,
                 gx,
             ).start()
-            return c
-
-        lax.fori_loop(1, owners, body, 0)
+
+        each_partner(send)
         rbuf[phase, h, me] = sbuf[phase, h, me]
 
     def exchange_sync(phase, h, sent):
@@ -180,6 +214,26 @@
     def hot(mask):
         return jnp.where(mask, 1.0, 0.0).astype(BF)
 
+    def index_level(level):
+        row, column, want = own_r[level], own_c[level], want_r[level]
+        down = lax.broadcasted_iota(jnp.int32, (routed, routed), 0)
+        across = lax.broadcasted_iota(jnp.int32, (routed, routed), 1)
+        same = row == column
+        rank_c = jnp.sum(jnp.where(same & (across < down), 1.0, 0.0), axis=1, keepdims=True)
+        rank_r = jnp.sum(jnp.where(same & (down < across), 1.0, 0.0), axis=0, keepdims=True)
+        rank_c, rank_r = rank_c.astype(jnp.int32), rank_r.astype(jnp.int32)
+        pos_r[level] = row * cap + rank_r
+        pos_c[level] = column * cap + rank_c
+        owner = lax.broadcasted_iota(jnp.int32, (owners, routed), 0)
+        high = lax.div(want, 32)
+        low_bits = (want - high * 32).astype(F32)
+        high = jnp.where(owner == row, high.astype(F32), 0.0).astype(BF)
+        low_bits = jnp.where(owner == row, low_bits, 0.0).astype(BF)
+        lane = lax.broadcasted_iota(jnp.int32, (routed, LANES), 1)
+        place = hot(lane == rank_c + level * SLOT_LANES)
+        chosen = dot(high, place) * 32.0 + dot(low_bits, place)
+        pick[...] = chosen if level == 0 else pick[...] + chosen
+
     def build_p(level):
         for c in range(slots // LANES):
             at = lax.broadcasted_iota(jnp.int32, (LANES, routed), 0) + c * LANES
@@ -192,15 +246,39 @@
             pt[level, span, :] = hot(at == pos_c[level, span, :])
 
     def build_s(level):
+        at = lax.broadcasted_iota(jnp.int32, (SLOT_LANES, slots), 0)
+        span = pl.ds(pl.multiple_of(level * SLOT_LANES, SLOT_LANES), SLOT_LANES)
+        lane = lax.broadcasted_iota(jnp.int32, (1, slots), 1)
+        own = lane - lax.div(lane, cap) * cap
+        row = jnp.sum(jnp.where(at == own, by_row[span, :], 0.0), axis=0, keepdims=True)
+        row = row.astype(jnp.int32)
         for c in range(sends * block // LANES):
             at = lax.broadcasted_iota(jnp.int32, (LANES, slots), 0) + (c * LANES + block + 1)
-            sm[level, pl.ds(c * LANES, LANES), :] = hot(at == idx_r[level])
+            sm[level, pl.ds(c * LANES, LANES), :] = hot(at == row)
 
     def build_g(level):
         for c in range(slots // LANES):
             span = pl.ds(c * LANES, LANES)
+            lane = lax.broadcasted_iota(jnp.int32, (LANES, LANES), 1)
+            order = lax.broadcasted_iota(jnp.int32, (LANES, 1), 0) + c * LANES
+            own = order - lax.div(order, cap) * cap + level * SLOT_LANES
+            column = jnp.sum(jnp.where(lane == own, by_col[span, :], 0.0), axis=1, keepdims=True)
             at = lax.broadcasted_iota(jnp.int32, (LANES, sends * block), 1) + (block + 1)
-            gm[level, span, :] = hot(at == idx_c[level, span, :])
+            gm[level, span, :] = hot(at == column.astype(jnp.int32))
+
+    def spread():
+        number = told[...].reshape(owners, LANES)
+        high = lax.div(number, 32)
+        low_bits = (number - high * 32).astype(F32).astype(BF)
+        high = high.astype(F32).astype(BF)
+        first = lax.broadcasted_iota(jnp.int32, (slots, owners), 0)
+        owner = lax.broadcasted_iota(jnp.int32, (slots, owners), 1) * cap
+        fan = hot((first >= owner) & (first < owner + cap))
+        by_col[...] = dot(fan, high) * 32.0 + dot(fan, low_bits)
+        first = lax.broadcasted_iota(jnp.int32, (owners, slots), 1)
+        owner = lax.broadcasted_iota(jnp.int32, (owners, slots), 0) * cap
+        fan = hot((first >= owner) & (first < owner + cap))
+        by_row[...] = dot_t(high, fan) * 32.0 + dot_t(low_bits, fan)
 
     def pack(phase, h, value):
         sbuf[phase, h] = value.astype(BF).reshape(owners, cap // 2, 2, LANES)
@@ -210,9 +288,21 @@
 
     for h in range(halves):
         blk[0, h, :, my_rows, :] = rhs[0, :, :, h * LANES : (h + 1) * LANES]
+    pl.semaphore_wait(barrier, others + groups - 1)
+    for h in range(halves):
         gather(0, h)
     matrix(0, finv, fwd_inv, fs, fr)
     columns(0)
+
+    for level in range(sends):
+        index_level(level)
+    asked[...] = pick[...].astype(jnp.int32).reshape(owners, 1, LANES)
+
+    def tell(to):
+        remote(asked.at[to], told.at[me], ix_s, ix_r, to, gx).start()
+
+    each_partner(tell)
+    told[me] = asked[me]
     my_columns = pl.ds(pl.multiple_of(gx * group_rows, group_rows), group_rows)
     for level in range(levels):
         finv[level, :, my_rows, :] = fwd_inv[level]
@@ -226,6 +316,9 @@
                 )
     for level in range(sends):
         build_p(level)
+    first = told.at[pl.ds(0, others)]
+    remote(first, first, ix_s, ix_r, lax.rem(me + 1, owners), gx).wait_recv()
+    spread()
 
     def lower(level, h):
         matrix_waited = []
@@ -336,6 +429,7 @@
         return c
 
     lax.fori_loop(0, levels, drain, 0)
+    remote(first, first, ix_s, ix_r, lax.rem(me + 1, owners), gx).wait_send()
 
     def drain_sends(level, c):
         matrix_sync(level, binv, bs, br, True)
@@ -369,16 +463,6 @@
 
     owner = by_supernode(dest_owner)
     target = by_supernode(dest_row)
-    order = jnp.arange(routed, dtype=jnp.int32)
-    same = (owner[:, :, None] == owner[:, None, :]) & (order[None, None, :] < order[None, :, None])
-    position = owner * cap + jnp.sum(same.astype(jnp.int32), axis=2)
-    slot_ids = jnp.arange(slots, dtype=jnp.int32)
-    chosen = slot_ids[None, :, None] == position[:, None, :]
-    asked = jnp.sum(jnp.where(chosen, target[:, None, :] + 1, 0), axis=2)
-    asked = jnp.swapaxes(asked.reshape(sends, owners, cap), 0, 1).reshape(owners, sends * cap)
-    told = lax.all_to_all(asked, "leaf", split_axis=0, concat_axis=0, tiled=True)
-    told = jnp.swapaxes(told.reshape(owners, sends, cap), 0, 1).reshape(sends, slots)
-
     dma = pltpu.SemaphoreType.DMA
     vmem = pltpu.VMEM
     sizes = (levels, per, rows, group_rows, owners, groups, cap, halves)
@@ -389,7 +473,7 @@
     return pl.pallas_call(
         body,
         out_shape=jax.ShapeDtypeStruct(rhs.shape, BF),
-        in_specs=[pl.BlockSpec(memory_space=vmem)] * 9,
+        in_specs=[pl.BlockSpec(memory_space=vmem)] * 8,
         out_specs=pl.BlockSpec(memory_space=vmem),
         scratch_shapes=[
             vmem((levels, per, width, width), BF),
@@ -408,6 +492,13 @@
             vmem((sends, routed, slots), BF),
             vmem((sends, sends * block, slots), BF),
             vmem((sends, slots, sends * block), BF),
+            vmem((owners, 1, LANES), jnp.int32),
+            vmem((LANES, slots), F32),
+            vmem((slots, LANES), F32),
+            vmem((owners, 1, LANES), jnp.int32),
+            vmem((owners, LANES), F32),
+            vmem((sends, 1, routed), jnp.int32),
+            vmem((sends, routed, 1), jnp.int32),
             dma((levels,)),
             dma((levels,)),
             dma((sends,)),
@@ -420,6 +511,8 @@
             dma((2 * sends, halves)),
             dma((sends, halves)),
             dma((sends, halves)),
+            dma,
+            dma,
         ],
         compiler_params=pltpu.CompilerParams(collective_id=0, has_side_effects=True),
     )(
@@ -428,10 +521,9 @@
         bwd_inv,
         upd_t,
         bwd_t,
-        position[:, None, :],
-        position[:, :, None],
-        told[:, None, :],
-        told[:, :, None],
+        owner[:, None, :],
+        owner[:, :, None],
+        target[:, None, :] + 1,
     )
 
 

time: 168 us -> 145 us (0.86)
  starting transfers between devices: 11.8 us -> 0 us
  waiting for transfers between devices: 6.81 us -> 0 us
  local copies, waits for them, and re-layouts: 7.25 us -> 4.47 us
    all_to_all x1 -> x0, starting transfers between devices: 11.8 us -> none  [local(): lax.all_to_all(asked, 'leaf', split_axis=0, concat_axis=0, tiled=True)]
    all_to_all x1 -> x0, waiting for transfers between devices: 6.81 us -> none  [local(): lax.all_to_all(asked, 'leaf', split_axis=0, concat_axis=0, tiled=True)]
  transfers between devices with their start and end apart: 1 -> 0, of which waited for: 1 -> 0; matrix products, arithmetic and copies ran while one was open for 1% -> 0% of each run, Pallas kernels for 0% -> 0%
where the time goes in v2:
time: 145 us; the launch traced here: 144 us
  Pallas kernels  139 us (96%)
  local copies, waits for them, and re-layouts  4.47 us (3%)
    pallas_call x1, Pallas kernels, local(): pl.pallas_call(body, out_shape=jax.ShapeDtypeStruct(rhs.shape, BF), in_sp...  139 us

profile of v2, /device:TPU:32, one launch (start us, length us, event | category | flops | bytes accessed | tf_op | source)
XLA Modules:
  0.0 144.4 jit_solution(13475755611689076567)
XLA Ops:
  0.0 0.7 broadcast_add_fusion
  0.7 0.1 copy.13
  0.8 0.0 copy-start
  0.8 0.7 copy.14
  1.5 0.0 copy-done
  1.5 0.1 copy.10
  1.7 0.1 copy.12
  1.7 0.7 copy.11
  2.4 1.0 copy.15.refs_6_
  3.5 139.2 %shard_map.73 = bf16[5,2,64,256]{3,2,1,0:T(8,128)(2,1)} custom-call(bf16[5,2,64,256]{3,2,1,0:T(8,128)(2,1)} %refs_0_.1, bf16[5,2,64,256]{3,2,1,0:T(8,128)(2,1)} %refs_1_.1, bf16[5,2,64,256]{3,2,1,0:T(8,128)(2,1)} %refs_2_.1, bf16[4,2,64,512]{3,2,1,0:T(8,128)(2,1)} %refs_3_.1, bf16[4,2,128,256]{3,2,1,0:T(8,128)(2,1)} %refs_4_.1, s32[4,1,256]{2,1,0:T(1,128)} %bitcast.13, ...), custom_call_target="tpu_custom_call" | custom-call | tf_op jit(solution)/shard_map/pallas_call | solution.py:473
  142.7 1.7 %copy.17 = bf16[5,2,64,256]{3,2,1,0:T(8,128)(2,1)} copy(bf16[5,2,64,256]{3,2,1,0:T(8,128)(2,1)} %shard_map.73) | data formatting | bytes 655360
Async XLA Ops:
  0.8 0.7 copy-start

commit v3 on v2

--- a/solution.py
+++ b/solution.py
@@ -11,6 +11,7 @@
 LANES = 128
 RING_Y, RING_Z, CORES = 4, 8, 2
 SLOT_LANES = 16
+FAR_FIRST = (2, 1, 3)
 
 
 def dot(a, b):
@@ -27,15 +28,14 @@
 
 def solve_kernel(
     sizes,
-    rhs,
+    rhs_in,
     fwd_inv,
-    bwd_inv,
+    bwd_in,
     upd,
-    bwd,
-    own_r,
-    own_c,
-    want_r,
-    out,
+    bwd_far,
+    owner_in,
+    target_in,
+    out_far,
     finv,
     binv,
     ucol,
@@ -73,6 +73,12 @@
     rd_r,
     ix_s,
     ix_r,
+    rhs,
+    bwd_inv,
+    bwd,
+    out,
+    in_sem,
+    out_sem,
 ):
     levels, per, rows, group_rows, owners, groups, cap, halves = sizes
     sends = levels - 1
@@ -133,11 +139,27 @@
     for step in range(1, groups):
         pl.semaphore_signal(barrier, inc=1, device_id=(me, peer(step)), device_id_type=MESH)
 
+    my_columns = pl.ds(pl.multiple_of(gx * group_rows, group_rows), group_rows)
+    loads = [
+        pltpu.make_async_copy(rhs_in, rhs, in_sem.at[0]),
+        pltpu.make_async_copy(bwd_in, bwd_inv, in_sem.at[1]),
+        pltpu.make_async_copy(bwd_far, bwd, in_sem.at[2]),
+        pltpu.make_async_copy(fwd_inv, finv.at[:, :, my_rows, :], in_sem.at[3]),
+        pltpu.make_async_copy(
+            bwd_in.at[pl.ds(0, sends)], binv.at[:, :, my_rows, :], in_sem.at[4]
+        ),
+        pltpu.make_async_copy(
+            upd.at[:, :, :, my_columns], ucol.at[:, :, my_rows, :], in_sem.at[5]
+        ),
+    ]
+    for load in loads:
+        load.start()
+
     def part(ref, count):
         return ref.at[:, pl.ds(0, count), :]
 
     def matrix(level, ref, mine, send, recv):
-        for step in range(1, groups):
+        for step in FAR_FIRST:
             remote(
                 mine.at[level],
                 ref.at[level, :, my_rows, :],
@@ -153,7 +175,7 @@
         copy.wait_send() if sent else copy.wait_recv()
 
     def columns(level):
-        for step in range(1, groups):
+        for step in FAR_FIRST:
             to = peer(step)
             remote(
                 upd.at[level, :, :, pl.ds(pl.multiple_of(to * group_rows, group_rows), group_rows)],
@@ -166,7 +188,7 @@
 
     def gather(level, h):
         view = blk.at[level, h, :, my_rows, :]
-        for step in range(1, groups):
+        for step in FAR_FIRST:
             remote(view, view, ag_s.at[level, h], ag_r.at[level, h], me, peer(step)).start()
 
     def gather_sync(level, h, sent):
@@ -195,7 +217,7 @@
         copy.wait_send() if sent else copy.wait_recv()
 
     def reduce_start(level, h):
-        for step in range(1, groups):
+        for step in FAR_FIRST:
             to = peer(step)
             remote(
                 rs_s.at[level, h, :, pl.ds(pl.multiple_of(to * rows, rows), rows), :],
@@ -215,9 +237,19 @@
         return jnp.where(mask, 1.0, 0.0).astype(BF)
 
     def index_level(level):
-        row, column, want = own_r[level], own_c[level], want_r[level]
         down = lax.broadcasted_iota(jnp.int32, (routed, routed), 0)
         across = lax.broadcasted_iota(jnp.int32, (routed, routed), 1)
+        supernode = lax.div(down, group_rows)
+        moved = across == (down - supernode * group_rows) * per + supernode
+
+        def turn(mask, values, axis):
+            return jnp.sum(jnp.where(mask, values, 0.0), axis=axis, keepdims=True)
+
+        column = turn(moved, owner_in[level].astype(F32), 1)
+        row = turn(down == across, column, 0)
+        want = turn(down == across, turn(moved, target_in[level].astype(F32), 1), 0)
+        row, column = row.astype(jnp.int32), column.astype(jnp.int32)
+        want = want.astype(jnp.int32) + 1
         same = row == column
         rank_c = jnp.sum(jnp.where(same & (across < down), 1.0, 0.0), axis=1, keepdims=True)
         rank_r = jnp.sum(jnp.where(same & (down < across), 1.0, 0.0), axis=0, keepdims=True)
@@ -286,29 +318,25 @@
     def unpack(phase, h):
         return rbuf[phase, h].reshape(slots, LANES)
 
+    loads[0].wait()
     for h in range(halves):
         blk[0, h, :, my_rows, :] = rhs[0, :, :, h * LANES : (h + 1) * LANES]
-    pl.semaphore_wait(barrier, others + groups - 1)
-    for h in range(halves):
-        gather(0, h)
-    matrix(0, finv, fwd_inv, fs, fr)
-    columns(0)
-
     for level in range(sends):
         index_level(level)
     asked[...] = pick[...].astype(jnp.int32).reshape(owners, 1, LANES)
+    told[me] = asked[me]
+    pl.semaphore_wait(barrier, others + groups - 1)
+    gather(0, 0)
+    matrix(0, finv, fwd_inv, fs, fr)
+    columns(0)
+    for h in range(1, halves):
+        gather(0, h)
 
     def tell(to):
         remote(asked.at[to], told.at[me], ix_s, ix_r, to, gx).start()
 
     each_partner(tell)
-    told[me] = asked[me]
-    my_columns = pl.ds(pl.multiple_of(gx * group_rows, group_rows), group_rows)
     for level in range(levels):
-        finv[level, :, my_rows, :] = fwd_inv[level]
-        if level < sends:
-            binv[level, :, my_rows, :] = bwd_inv[level]
-            ucol[level, :, my_rows, :] = upd[level, :, :, my_columns]
         if level > 0:
             for h in range(halves):
                 acc[level, h] = (
@@ -319,6 +347,8 @@
     first = told.at[pl.ds(0, others)]
     remote(first, first, ix_s, ix_r, lax.rem(me + 1, owners), gx).wait_recv()
     spread()
+    for load in loads[1:]:
+        load.wait()
 
     def lower(level, h):
         matrix_waited = []
@@ -347,7 +377,7 @@
 
         @pl.when(level == sends - 1)
         def _():
-            matrix(sends - 1, binv, bwd_inv, bs, br)
+            matrix(sends - 1, binv, bwd_in, bs, br)
 
         build_s(level)
         build_g(level)
@@ -383,6 +413,9 @@
         sol[h, pl.ds(at, rows), :] = result
         out[level, k, :, h * LANES : (h + 1) * LANES] = result
 
+    def leave(level):
+        return pltpu.make_async_copy(out.at[level], out_far.at[level], out_sem.at[level])
+
     sol[...] = jnp.zeros(sol.shape, BF)
     matrix_sync(sends, finv, fs, fr, False)
     for h in range(halves):
@@ -390,6 +423,7 @@
         lowered = lower(sends, h)
         for k in range(per):
             finish(sends, h, k, dot(bwd_inv[sends, k], lowered[k]))
+    leave(sends).start()
 
     def backward(i, c):
         level = sends - 1 - i
@@ -401,7 +435,7 @@
 
         @pl.when(level > 0)
         def _():
-            matrix(level - 1, binv, bwd_inv, bs, br)
+            matrix(level - 1, binv, bwd_in, bs, br)
 
         matrix_sync(level, binv, bs, br, False)
         for h in range(halves):
@@ -418,6 +452,7 @@
                 for step in range(1, groups):
                     total = total + rs_r[level, h, peer(step), k].astype(F32)
                 finish(level, h, k, const[level, h, k] - total)
+        leave(level).start()
         return c
 
     lax.fori_loop(0, sends, backward, 0)
@@ -426,6 +461,7 @@
         matrix_sync(level, finv, fs, fr, True)
         for h in range(halves):
             gather_sync(level, h, True)
+        leave(level).wait()
         return c
 
     lax.fori_loop(0, levels, drain, 0)
@@ -457,12 +493,6 @@
     block = per * rows
     width = rows * groups
 
-    def by_supernode(index):
-        split = index.reshape(sends, group_rows, per)
-        return jnp.swapaxes(split, 1, 2).reshape(sends, routed)
-
-    owner = by_supernode(dest_owner)
-    target = by_supernode(dest_row)
     dma = pltpu.SemaphoreType.DMA
     vmem = pltpu.VMEM
     sizes = (levels, per, rows, group_rows, owners, groups, cap, halves)
@@ -473,8 +503,9 @@
     return pl.pallas_call(
         body,
         out_shape=jax.ShapeDtypeStruct(rhs.shape, BF),
-        in_specs=[pl.BlockSpec(memory_space=vmem)] * 8,
-        out_specs=pl.BlockSpec(memory_space=vmem),
+        in_specs=[pl.BlockSpec(memory_space=pl.ANY)] * 5
+        + [pl.BlockSpec(memory_space=vmem)] * 2,
+        out_specs=pl.BlockSpec(memory_space=pl.ANY),
         scratch_shapes=[
             vmem((levels, per, width, width), BF),
             vmem((sends, per, width, width), BF),
@@ -513,6 +544,12 @@
             dma((sends, halves)),
             dma,
             dma,
+            vmem(rhs.shape, BF),
+            vmem(bwd_inv.shape, BF),
+            vmem(bwd_t.shape, BF),
+            vmem(rhs.shape, BF),
+            dma((6,)),
+            dma((levels,)),
         ],
         compiler_params=pltpu.CompilerParams(collective_id=0, has_side_effects=True),
     )(
@@ -521,9 +558,8 @@
         bwd_inv,
         upd_t,
         bwd_t,
-        owner[:, None, :],
-        owner[:, :, None],
-        target[:, None, :] + 1,
+        dest_owner.reshape(sends, 1, routed),
+        dest_row.reshape(sends, 1, routed),
     )
 
 

time: 145 us -> 138 us (0.952)
  Pallas kernels: 139 us -> 136 us
  local copies, waits for them, and re-layouts: 4.47 us -> 1.72 us
    pallas_call x1, Pallas kernels: 139 us -> 136 us  [local(): pl.pallas_call(body, out_shape=jax.ShapeDtypeStruct(rhs.shape, BF), in_sp...]
where the time goes in v3:
time: 138 us; the launch traced here: 137 us
  Pallas kernels  136 us (99%)
  local copies, waits for them, and re-layouts  1.72 us (1%)
    pallas_call x1, Pallas kernels, local(): pl.pallas_call(body, out_shape=jax.ShapeDtypeStruct(rhs.shape, BF), in_sp...  136 us

profile of v3, /device:TPU:32, one launch (start us, length us, event | category | flops | bytes accessed | tf_op | source)
XLA Modules:
  0.0 137.5 jit_solution(4140100760104787948)
XLA Ops:
  0.0 135.8 %shard_map.73 = bf16[5,2,64,256]{3,2,1,0:T(8,128)(2,1)} custom-call(bf16[5,2,64,256]{3,2,1,0:T(8,128)(2,1)} %refs_0_.1, bf16[5,2,64,256]{3,2,1,0:T(8,128)(2,1)} %refs_1_.1, bf16[5,2,64,256]{3,2,1,0:T(8,128)(2,1)} %refs_2_.1, bf16[4,2,64,512]{3,2,1,0:T(8,128)(2,1)} %refs_3_.1, bf16[4,2,128,256]{3,2,1,0:T(8,128)(2,1)} %refs_4_.1, s32[4,1,256]{2,1,0:T(1,128)} %bitcast.2, ...), custom_call_target="tpu_custom_call" | custom-call | tf_op jit(solution)/shard_map/pallas_call | solution.py:503
  135.8 1.7 %copy.9 = bf16[5,2,64,256]{3,2,1,0:T(8,128)(2,1)} copy(bf16[5,2,64,256]{3,2,1,0:T(8,128)(2,1)} %shard_map.73) | data formatting | bytes 655360

commit v4 on v3

--- a/solution.py
+++ b/solution.py
@@ -369,7 +369,8 @@
             packed = dot(pm[level], jnp.concatenate(summed, axis=0))
             pack(level, h, packed)
             exchange(level, h)
-        matrix(level + 1, finv, fwd_inv, fs, fr)
+            if h == 0:
+                matrix(level + 1, finv, fwd_inv, fs, fr)
 
         @pl.when(level < sends - 1)
         def _():

time: 138 us -> 138 us (level)
  no operation moved by 1% of the time
where the time goes in v4:
time: 138 us; the launch traced here: 137 us
  Pallas kernels  136 us (99%)
  local copies, waits for them, and re-layouts  1.72 us (1%)
    pallas_call x1, Pallas kernels, local(): pl.pallas_call(body, out_shape=jax.ShapeDtypeStruct(rhs.shape, BF), in_sp...  136 us

profile of v4, /device:TPU:32, one launch (start us, length us, event | category | flops | bytes accessed | tf_op | source)
XLA Modules:
  0.0 137.4 jit_solution(10494941089583406887)
XLA Ops:
  0.0 135.6 %shard_map.73 = bf16[5,2,64,256]{3,2,1,0:T(8,128)(2,1)} custom-call(bf16[5,2,64,256]{3,2,1,0:T(8,128)(2,1)} %refs_0_.1, bf16[5,2,64,256]{3,2,1,0:T(8,128)(2,1)} %refs_1_.1, bf16[5,2,64,256]{3,2,1,0:T(8,128)(2,1)} %refs_2_.1, bf16[4,2,64,512]{3,2,1,0:T(8,128)(2,1)} %refs_3_.1, bf16[4,2,128,256]{3,2,1,0:T(8,128)(2,1)} %refs_4_.1, s32[4,1,256]{2,1,0:T(1,128)} %bitcast.2, ...), custom_call_target="tpu_custom_call" | custom-call | tf_op jit(solution)/shard_map/pallas_call | solution.py:504
  135.6 1.7 %copy.9 = bf16[5,2,64,256]{3,2,1,0:T(8,128)(2,1)} copy(bf16[5,2,64,256]{3,2,1,0:T(8,128)(2,1)} %shard_map.73) | data formatting | bytes 655360
